TPU v7x, 32 devices: a whole 2x2x4 slice. The times are simulated.
32 devices in a mesh: space: 4 (over y, x), snap: 8 (over z, core).
Axes of the slice: x: 2, y: 2, z: 4, core: 2. Of those that a mesh axis runs over, the one named last changes fastest.
Arguments:
- snapshots: bfloat16 [4096, 32768], P('space', 'snap'), may hold values from -6 to 6
- vectors_cyclic: float32 [32768, 64], P('snap', 'space'), may hold values from -0.03125 to 0.03125
- eigen_values: float32 [64], replicated, may hold values from 0.25 to 25
- held_out: bfloat16 [4096, 256], P(('space', 'snap')), may hold values from -6 to 6
Outputs:
- modes: bfloat16 [4096, 64], P(('space', 'snap'))
- coefficients: float32 [64, 256], replicated
All inputs are finite; a program needn't handle non-finite values.
Results may differ from a plain program's by a relative error of at most 0.0052.
Values sent between devices are 32-bit elements; how exact they have to be, the bound alone decides.
No kernel may reach another device: no remote copies, remote signals or barrier semaphores. Data moves between devices by JAX's collectives and lax.ppermute only.
A program may use at most 64 MiB of HBM per device.

v0:
```python
import math
import jax
import jax.numpy as jnp
from jax import lax
from jax.sharding import PartitionSpec as P

ROW_BLOCK = 16
COL_BLOCK = 4


def order_rows(received, snap_count):
    slab_rows, width = received.shape
    blocks_each = slab_rows // (snap_count * ROW_BLOCK)
    shaped = received.reshape(snap_count, blocks_each, ROW_BLOCK, width)
    return shaped.transpose(1, 0, 2, 3).reshape(slab_rows, width)


def order_columns(gathered, space_count):
    slab_rows, width = gathered.shape
    shaped = gathered.reshape(slab_rows, space_count, width // (space_count * COL_BLOCK), COL_BLOCK)
    return shaped.transpose(0, 2, 1, 3).reshape(slab_rows, width)


def per_device(snapshots, vectors_cyclic, eigen_values, held_out):
    snap_count = lax.axis_size("snap")
    space_count = lax.axis_size("space")
    moved = lax.all_to_all(vectors_cyclic, "snap", split_axis=0, concat_axis=0, tiled=True)
    moved = order_rows(moved, snap_count)
    widened = lax.all_gather(moved, "space", axis=1, tiled=True)
    eigvec = order_columns(widened, space_count)
    scaled = (eigvec * lax.rsqrt(eigen_values)[None, :]).astype(jnp.bfloat16)
    summed = lax.psum_scatter(
        jnp.dot(snapshots, scaled, preferred_element_type=jnp.float32),
        "snap",
        scatter_dimension=0,
        tiled=True,
    )
    modes = summed.astype(jnp.bfloat16)
    total_cells = snapshots.shape[0] * space_count
    partial_value = lax.dot_general(
        modes, held_out, (((0,), (0,)), ((), ())), preferred_element_type=jnp.float32
    )
    coefficients = lax.psum(partial_value, ("space", "snap")) / math.sqrt(total_cells)
    return (modes, coefficients)


def solution(mesh):
    return jax.shard_map(
        per_device,
        mesh=mesh,
        in_specs=(P("space", "snap"), P("snap", "space"), P(), P(("space", "snap"), None)),
        out_specs=(P(("space", "snap"), None), P()),
        check_vma=False,
    )
```

profile of v0, /device:TPU:1, one launch (start us, length us, event | category | flops | bytes accessed | tf_op | source)
XLA Modules:
  0.0 229.9 jit_solution(1001698393581418239)
XLA Ops:
  7.2 0.0 copy-start
  7.2 0.0 copy-start.2
  7.2 0.0 all-gather.2.cloned.1.call-start
  7.2 1.0 copy.11
  8.2 14.8 %all_to_all.9 = f32[8,512,16]{1,2,0:T(8,128)S(1)} all-to-all(f32[8,512,16]{1,2,0:T(8,128)S(1)} %bitcast.23), channel_id=1, replica_groups=mesh['space'=4,'snap'=8] {'snap'}, dimensions={0} | all-to-all | bytes 524288 | tf_op jit(solution)/shard_map/all_to_all | solution.py:27
  23.0 0.7 reshape.20
  23.8 3.0 %copy.7 = f32[32,8,16,16]{2,1,0,3:T(8,128)} copy(f32[32,8,16,16]{2,0,3,1:T(8,128)S(1)} %bitcast.21) | data formatting | bytes 524288 | tf_op jit(solution)/shard_map/transpose | solution.py:15
  26.8 3.8 %reshape.21 = f32[4096,16]{0,1:T(8,128)} reshape(f32[32,8,16,16]{2,1,0,3:T(8,128)} %copy.7) | data formatting | bytes 524288 | tf_op jit(solution)/shard_map/reshape | solution.py:15
  30.6 0.0 all-gather.2.cloned.1.call-update
  30.6 0.0 reduce-scatter.2.cloned.1.call-start
  30.7 0.0 copy-done.2
  30.7 25.7 %all-gather.2.cloned.1.call-done = f32[4096,64]{0,1:T(8,128)} async-done(((f32[4096,16]{0,1:T(8,128)}), f32[4096,64]{0,1:T(8,128)}) %all-gather.2.cloned.1.call-update) | async-done | bytes 1048592 | tf_op jit(solution)/shard_map/all_gather | solution.py:29
  56.4 1.5 reshape.22
  57.9 0.1 copy.8
  58.0 0.4 reshape.23
  58.4 6.8 %convolution_bitcast_fusion = f32[1024,64]{0,1:T(8,128)} fusion(bf16[1024,4096]{1,0:T(8,128)(2,1)} %param.4, f32[4096,64]{0,1:T(8,128)S(1)} %reshape.23, f32[64]{0:T(128)S(1)} %rsqrt.3), kind=kOutput, calls=%fused_computation | convolution fusion | flops 537395200 | bytes 9699584 | tf_op jit(solution)/shard_map/dot_general | solution.py:33
  65.2 0.0 reduce-scatter.2.cloned.1.call-update
  65.2 0.0 all-reduce.2.cloned.1.call-start
  65.3 27.7 %reduce-scatter.2.cloned.1.call-done = f32[128,64]{0,1:T(8,128)} async-done(((f32[1024,64]{0,1:T(8,128)}), f32[128,64]{0,1:T(8,128)}) %reduce-scatter.2.cloned.1.call-update) | async-done | bytes 32784 | tf_op jit(solution)/shard_map/reduce_scatter | solution.py:32
  93.0 0.8 convert_element_type.7
  93.8 0.0 copy-done
  93.8 0.0 copy-start.1
  93.8 0.8 fusion.1
  94.5 0.0 all-reduce.2.cloned.1.call-update
  94.6 127.4 %all-reduce.2.cloned.1.call-done = f32[64,256]{1,0:T(8,128)} async-done(((f32[64,256]{1,0:T(8,128)}), f32[64,256]{1,0:T(8,128)}) %all-reduce.2.cloned.1.call-update) | async-done | bytes 65552 | tf_op jit(solution)/shard_map/psum | solution.py:43
  221.9 1.5 broadcast_multiply_fusion
  223.4 0.0 copy-done.1
  (1 shorter events, 0.0 us)
Async XLA Ops:
  7.2 86.6 %copy-start = (bf16[128,256]{1,0:T(8,128)(2,1)S(1)}, bf16[128,256]{1,0:T(8,128)(2,1)}, u32[]{:S(2)}) copy-start(bf16[128,256]{1,0:T(8,128)(2,1)} %param.7) | copy-start | bytes 196612
  7.2 23.5 %copy-start.2 = (f32[64]{0:T(128)S(1)}, f32[64]{0:T(128)}, u32[]{:S(2)}) copy-start(f32[64]{0:T(128)} %param.6) | copy-start | bytes 772
  7.2 49.2 %all-gather.2.cloned.1.call-start = ((), (), s32[]{:S(2)}) async-start(), calls=%async_computation.2 | async-start | bytes 1310720 | tf_op jit(solution)/shard_map/all_gather | solution.py:29
  30.6 62.4 %reduce-scatter.2.cloned.1.call-start = ((), (), s32[]{:S(2)}) async-start(), calls=%async_computation.3 | async-start | bytes 294912 | tf_op jit(solution)/shard_map/reduce_scatter | solution.py:32
  65.2 156.7 %all-reduce.2.cloned.1.call-start = ((), (), s32[]{:S(2)}) async-start(), calls=%async_computation.4 | async-start | bytes 131072 | tf_op jit(solution)/shard_map/psum | solution.py:43
  93.8 129.6 %copy-start.1 = (bf16[128,64]{0,1:T(8,128)(2,1)}, bf16[128,64]{0,1:T(8,128)(2,1)S(1)}, u32[]{:S(2)}) copy-start(bf16[128,64]{0,1:T(8,128)(2,1)S(1)} %convert_element_type.7) | copy-start | bytes 49156
Sparse Core Ops, SparseCore 0:
  30.7 25.6 all-gather.1
  65.3 27.6 reduce-scatter.1
  99.2 122.7 all-reduce.1
where the time goes:
time: 230 us
  waiting for transfers between devices  181 us (79%)
  blocking collectives  14.8 us (6%)
  between operations  13.8 us (6%)
  local copies, waits for them, and re-layouts  10.5 us (5%)
  matrix products  7.53 us (3%)
    psum x1, waiting for transfers between devices, per_device(): lax.psum(partial_value, ('space', 'snap')) / math.sqrt(total_cells)  127 us
    reduce_scatter x1, waiting for transfers between devices, per_device(): lax.psum_scatter(jnp.dot(snapshots, scaled, preferred_element_type=jnp.fl...  27.7 us
    all_gather x1, waiting for transfers between devices, per_device(): widened = lax.all_gather(moved, 'space', axis=1, tiled=True)  25.7 us
    all_to_all x1, blocking collectives, per_device(): lax.all_to_all(vectors_cyclic, 'snap', split_axis=0, concat_axis=0, tiled...  14.8 us
    dot_general x1, matrix products, per_device(): jnp.dot(snapshots, scaled, preferred_element_type=jnp.float32)  6.77 us
  transfers between devices with their start and end apart: 3, of which 3 were waited for; matrix products, arithmetic and copies ran while one was open for 0% of the time, Pallas kernels for 0%

commit v1 on v0

--- a/solution.py
+++ b/solution.py
@@ -40,7 +40,9 @@
     partial_value = lax.dot_general(
         modes, held_out, (((0,), (0,)), ((), ())), preferred_element_type=jnp.float32
     )
-    coefficients = lax.psum(partial_value, ("space", "snap")) / math.sqrt(total_cells)
+    coefficients = jnp.sum(lax.all_gather(partial_value, ("space", "snap")), axis=0) / math.sqrt(
+        total_cells
+    )
     return (modes, coefficients)
 
 

time: 230 us -> 164 us (0.71)
  waiting for transfers between devices: 181 us -> 114 us
    psum x1 -> x0, waiting for transfers between devices: 127 us -> none  [per_device(): lax.psum(partial_value, ('space', 'snap')) / math.sqrt(total_cells)]
    all_gather x0 -> x1, waiting for transfers between devices: none -> 60.3 us  [per_device(): lax.all_gather(partial_value, ('space', 'snap'))]
where the time goes in v1:
time: 164 us
  waiting for transfers between devices  114 us (70%)
  blocking collectives  14.8 us (9%)
  between operations  13.8 us (8%)
  local copies, waits for them, and re-layouts  10.5 us (6%)
  matrix products  7.53 us (5%)
  other arithmetic  3.11 us (2%)
    all_gather x1, waiting for transfers between devices, per_device(): lax.all_gather(partial_value, ('space', 'snap'))  60.3 us
    reduce_scatter x1, waiting for transfers between devices, per_device(): lax.psum_scatter(jnp.dot(snapshots, scaled, preferred_element_type=jnp.fl...  27.7 us
    all_gather x1, waiting for transfers between devices, per_device(): widened = lax.all_gather(moved, 'space', axis=1, tiled=True)  25.7 us
    all_to_all x1, blocking collectives, per_device(): lax.all_to_all(vectors_cyclic, 'snap', split_axis=0, concat_axis=0, tiled...  14.8 us
    dot_general x1, matrix products, per_device(): jnp.dot(snapshots, scaled, preferred_element_type=jnp.float32)  6.77 us
    reshape x1, local copies, waits for them, and re-layouts, order_rows(): return shaped.transpose(1, 0, 2, 3).reshape(slab_rows, width)  3.84 us
  transfers between devices with their start and end apart: 3, of which 3 were waited for; matrix products, arithmetic and copies ran while one was open for 0% of the time, Pallas kernels for 0%

profile of v1, /device:TPU:1, one launch (start us, length us, event | category | flops | bytes accessed | tf_op | source)
XLA Modules:
  0.0 163.7 jit_solution(8230699494446152416)
XLA Ops:
  7.2 0.0 copy-start
  7.2 0.0 copy-start.2
  7.2 0.0 all-gather.4.cloned.1.call-start
  7.2 1.0 copy.11
  8.2 14.8 %all_to_all.9 = f32[8,512,16]{1,2,0:T(8,128)S(1)} all-to-all(f32[8,512,16]{1,2,0:T(8,128)S(1)} %bitcast.25), channel_id=1, replica_groups=mesh['space'=4,'snap'=8] {'snap'}, dimensions={0} | all-to-all | bytes 524288 | tf_op jit(solution)/shard_map/all_to_all | solution.py:27
  23.0 0.7 reshape.20
  23.8 3.0 %copy.7 = f32[32,8,16,16]{2,1,0,3:T(8,128)} copy(f32[32,8,16,16]{2,0,3,1:T(8,128)S(1)} %bitcast.22) | data formatting | bytes 524288 | tf_op jit(solution)/shard_map/transpose | solution.py:15
  26.8 3.8 %reshape.21 = f32[4096,16]{0,1:T(8,128)} reshape(f32[32,8,16,16]{2,1,0,3:T(8,128)} %copy.7) | data formatting | bytes 524288 | tf_op jit(solution)/shard_map/reshape | solution.py:15
  30.6 0.0 all-gather.4.cloned.1.call-update
  30.6 0.0 reduce-scatter.2.cloned.1.call-start
  30.7 0.0 copy-done.2
  30.7 25.7 %all-gather.4.cloned.1.call-done = f32[4096,64]{0,1:T(8,128)} async-done(((f32[4096,16]{0,1:T(8,128)}), f32[4096,64]{0,1:T(8,128)}) %all-gather.4.cloned.1.call-update) | async-done | bytes 1048592 | tf_op jit(solution)/shard_map/all_gather | solution.py:29
  56.4 1.5 reshape.22
  57.9 0.1 copy.8
  58.0 0.4 reshape.23
  58.4 6.8 %convolution_bitcast_fusion = f32[1024,64]{0,1:T(8,128)} fusion(bf16[1024,4096]{1,0:T(8,128)(2,1)} %param.4, f32[4096,64]{0,1:T(8,128)S(1)} %reshape.23, f32[64]{0:T(128)S(1)} %rsqrt.3), kind=kOutput, calls=%fused_computation | convolution fusion | flops 537395200 | bytes 9699584 | tf_op jit(solution)/shard_map/dot_general | solution.py:33
  65.2 0.0 reduce-scatter.2.cloned.1.call-update
  65.2 0.0 all-gather.6.cloned.1.call-start
  65.3 27.7 %reduce-scatter.2.cloned.1.call-done = f32[128,64]{0,1:T(8,128)} async-done(((f32[1024,64]{0,1:T(8,128)}), f32[128,64]{0,1:T(8,128)}) %reduce-scatter.2.cloned.1.call-update) | async-done | bytes 32784 | tf_op jit(solution)/shard_map/reduce_scatter | solution.py:32
  93.0 0.8 convert_element_type.7
  93.8 0.0 copy-done
  93.8 0.0 copy-start.1
  93.8 0.8 fusion.1
  94.5 0.0 all-gather.6.cloned.1.call-update
  94.6 60.3 %all-gather.6.cloned.1.call-done = f32[2048,256]{1,0:T(8,128)} async-done(((f32[64,256]{1,0:T(8,128)}), f32[2048,256]{1,0:T(8,128)}) %all-gather.6.cloned.1.call-update) | async-done | bytes 2097168 | tf_op jit(solution)/shard_map/all_gather | solution.py:43
  154.9 1.7 %reduce_sum.9 = f32[64,256]{1,0:T(8,128)S(1)} reduce(f32[32,64,256]{2,1,0:T(8,128)} %bitcast.24, f32[]{:T(128)} %constant.1.clone.1), dimensions={0}, to_apply=%region_1.0 | reduce | flops 507904 | bytes 2162692 | tf_op jit(solution)/shard_map/reduce_sum | solution.py:43
  156.6 0.6 broadcast_multiply_fusion
  157.2 0.0 copy-done.1
  (1 shorter events, 0.0 us)
Async XLA Ops:
  7.2 86.6 %copy-start = (bf16[128,256]{1,0:T(8,128)(2,1)S(1)}, bf16[128,256]{1,0:T(8,128)(2,1)}, u32[]{:S(2)}) copy-start(bf16[128,256]{1,0:T(8,128)(2,1)} %param.7) | copy-start | bytes 196612
  7.2 23.5 %copy-start.2 = (f32[64]{0:T(128)S(1)}, f32[64]{0:T(128)}, u32[]{:S(2)}) copy-start(f32[64]{0:T(128)} %param.6) | copy-start | bytes 772
  7.2 49.2 %all-gather.4.cloned.1.call-start = ((), (), s32[]{:S(2)}) async-start(), calls=%async_computation.2 | async-start | bytes 1310720 | tf_op jit(solution)/shard_map/all_gather | solution.py:29
  30.6 62.4 %reduce-scatter.2.cloned.1.call-start = ((), (), s32[]{:S(2)}) async-start(), calls=%async_computation.3 | async-start | bytes 294912 | tf_op jit(solution)/shard_map/reduce_scatter | solution.py:32
  65.2 89.6 %all-gather.6.cloned.1.call-start = ((), (), s32[]{:S(2)}) async-start(), calls=%async_computation.4 | async-start | bytes 2162688 | tf_op jit(solution)/shard_map/all_gather | solution.py:43
  93.8 63.4 %copy-start.1 = (bf16[128,64]{0,1:T(8,128)(2,1)}, bf16[128,64]{0,1:T(8,128)(2,1)S(1)}, u32[]{:S(2)}) copy-start(bf16[128,64]{0,1:T(8,128)(2,1)S(1)} %convert_element_type.7) | copy-start | bytes 49156
Sparse Core Ops, SparseCore 0:
  30.7 25.6 all-gather.3
  65.3 27.6 reduce-scatter.1
  96.6 58.2 all-gather.5
